TPU v7x, 512 devices: a whole 4x8x8 slice. The times are simulated.
512 devices in a mesh: leaf: 8 (over z), row: 8 (over y_lo, x), col: 8 (over y_hi, core).
Axes of the slice: x: 4, y: 8 (y_hi: 4, y_lo: 2; y = y_hi * 2 + y_lo), z: 8, core: 2. Of those that a mesh axis runs over, the one named last changes fastest.
Arguments:
- child_update: bfloat16 [8, 3072, 3072], P('leaf', 'row', 'col'), as said below
- block_map: int32 [8, 24], replicated, may hold values from 0 to 63, as said below
- pivot_entries: float32 [8, 4096, 512], P('leaf', 'row'), as said below
- pivot_count: int32 [4], replicated, may hold values from 256 to 512, as said below
Outputs:
- factor: float32 [8, 4096, 512], P('leaf', 'row')
- update: bfloat16 [8, 4096, 8192], P('leaf', 'row', 'col')
Inputs may be any that keep to these rules, and one draw needn't show every extreme that they name: `child_update`: each child's block is symmetric positive definite. `block_map`: each row lists 3072/128 distinct parent blocks in increasing order and includes the first and the last block; rows of odd children list, besides the first block, only blocks from 32 on. `pivot_entries`: the first 512 rows of each even leaf slice form a symmetric positive definite block. `pivot_count`: some parent has exactly 512 pivots.
All inputs are finite; a program needn't handle non-finite values.
Results may differ from a plain program's by a relative error of at most 0.01.
Values may be sent and summed in bfloat16 or wider, within the bound.
A program may use at most 64 MiB of HBM per device.

v0:
```python
import jax
import jax.numpy as jnp
from jax import lax
from jax.sharding import PartitionSpec as P

NF = 8192
BLK = 128
PMAX = 512


def from_partner(shard, axis, apart):
    return lax.ppermute(shard, axis, [(i, i ^ 1 << apart) for i in range(lax.axis_size(axis))])


def spread(value, axis, source):
    kept = jnp.where(lax.axis_index(axis) == source, value, 0).astype(value.dtype)
    return lax.psum(kept, axis)


def source_index(block_list, targets):
    matches = block_list[None, :] == (targets // BLK)[:, None]
    present = jnp.any(matches, axis=1)
    slots = jnp.arange(block_list.shape[0], dtype=jnp.int32)
    position = jnp.sum(jnp.where(matches, slots[None, :], 0), axis=1)
    return jnp.where(present, position * BLK + targets % BLK, -1)


def pick_entries(shard_piece, sources, along):
    extent = shard_piece.shape[along]
    inside = (sources >= 0) & (sources >= 0) & (sources < extent)
    picked = jnp.take(shard_piece, jnp.clip(sources, 0, extent - 1), axis=along).astype(jnp.float32)
    shaped = inside[:, None] if along == 0 else inside[None, :]
    return jnp.where(shaped, picked, 0.0)


def solve_rows(pivot_square, columns, pivot_mask):
    pivot_pair = pivot_mask[:, None] & pivot_mask[None, :]
    square = jnp.where(pivot_pair, pivot_square, jnp.eye(PMAX, dtype=jnp.float32))
    chol_lower = jnp.linalg.cholesky(square)
    return lax.linalg.triangular_solve(
        chol_lower, columns, left_side=False, lower=True, transpose_a=True
    )


def on_device(child_update, block_map, pivot_entries, pivot_count):
    leaf_id = lax.axis_index("leaf")
    half_id = leaf_id % 2
    parent_id = leaf_id // 2
    row_count = lax.axis_size("row")
    col_count = lax.axis_size("col")
    row_id = lax.axis_index("row")
    col_id = lax.axis_index("col")
    child_block = child_update[0]
    own_map = block_map[leaf_id]
    owner_rows = pivot_entries.shape[1]
    range_cols = NF // col_count
    half_rows = NF // 2
    steps_rows = jnp.arange(owner_rows, dtype=jnp.int32)
    row_targets = jnp.concatenate(
        [row_id * owner_rows + steps_rows, half_rows + row_id * owner_rows + steps_rows]
    )
    col_targets = col_id * range_cols + jnp.arange(range_cols, dtype=jnp.int32)
    row_sources = source_index(own_map, row_targets)
    col_sources = source_index(own_map, col_targets)
    strip = pick_entries(lax.all_gather(child_block, "col", axis=1, tiled=True), col_sources, 1)
    both_halves = pick_entries(
        lax.all_gather(strip.astype(jnp.bfloat16), "row", axis=0, tiled=True), row_sources, 0
    )
    both_halves = both_halves.astype(jnp.bfloat16)
    own_half = jnp.where(half_id == 0, both_halves[:owner_rows], both_halves[owner_rows:])
    other_half = jnp.where(half_id == 0, both_halves[owner_rows:], both_halves[:owner_rows])
    from_sibling = from_partner(other_half, "leaf", 0)
    assembled = own_half.astype(jnp.float32) + from_sibling.astype(jnp.float32)
    pivots = pivot_count[parent_id]
    pivot_mask = jnp.arange(PMAX, dtype=jnp.int32) < pivots
    local_columns = jnp.where(pivot_mask[None, :], assembled[:, :PMAX] + pivot_entries[0], 0.0)
    received = (
        from_partner(local_columns.astype(jnp.bfloat16), "leaf", 0).astype(local_columns.dtype),
        from_partner(local_columns.astype(jnp.bfloat16), "leaf", 0).astype(local_columns.dtype),
    )
    square_piece = jnp.where(half_id == 0, local_columns, received[0])
    lower_rows = jnp.where(half_id == 0, local_columns, received[1])
    upper_rows = jnp.where(half_id == 0, received[1], local_columns)
    pair_columns = jnp.concatenate([lower_rows, upper_rows], axis=0)
    pivot_square = spread(square_piece.astype(jnp.bfloat16), "row", 0).astype(square_piece.dtype)
    factor_pair = spread(solve_rows(pivot_square, pair_columns, pivot_mask), "col", 0)
    factor_rows = jnp.where(half_id == 0, factor_pair[:owner_rows], factor_pair[owner_rows:])
    rounded_pair = factor_pair.astype(jnp.bfloat16)
    rounded = jnp.where(half_id == 0, rounded_pair[:owner_rows], rounded_pair[owner_rows:])
    per_range = range_cols // owner_rows
    first_owner = col_id * per_range
    owner_half = first_owner // row_count
    range_source = jnp.where(owner_half == 0, rounded_pair[:owner_rows], rounded_pair[owner_rows:])
    gathered = []
    for part_id in range(per_range):
        gathered.append(spread(range_source, "row", (first_owner + part_id) % row_count))
    far_rows = jnp.concatenate(gathered, axis=0)
    product = lax.dot_general(
        rounded, far_rows, (((1,), (1,)), ((), ())), preferred_element_type=jnp.float32
    )
    schur_part = assembled - product
    row_true = half_id * half_rows + row_id * owner_rows + steps_rows
    keep_rows = row_true >= pivots
    keep_cols = col_targets >= pivots
    update = jnp.where(keep_rows[:, None] & keep_cols[None, :], schur_part, 0.0).astype(
        jnp.bfloat16
    )
    return (factor_rows[None], update[None])


def solution(mesh):
    return jax.shard_map(
        on_device,
        mesh=mesh,
        in_specs=(P("leaf", "row", "col"), P(), P("leaf", "row", None), P()),
        out_specs=(P("leaf", "row", None), P("leaf", "row", "col")),
        check_vma=False,
    )
```

profile of v0, /device:TPU:16, one launch (start us, length us, event | category | flops | bytes accessed | tf_op | source)
XLA Modules:
  0.0 648.8 jit_solution(12378663692728715487)
XLA Ops:
  7.2 1.8 copy.38
  9.6 45.9 %all-gather.6.cloned.1.call-done = bf16[1,384,3072]{1,2,0:T(8,128)(2,1)} async-done(((bf16[1,384,384]{1,2,0:T(8,128)(2,1)}), bf16[1,384,3072]{1,2,0:T(8,128)(2,1)}) %all-gather.6.cloned.1.call-update) | async-done | bytes 2359312 | tf_op jit(solution)/shard_map/all_gather | solution.py:65
  55.5 5.7 gather_fusion
  61.2 1.2 fusion.17
  62.6 75.8 %all-gather.4.cloned.1.call-done = bf16[3072,1024]{0,1:T(8,128)(2,1)} async-done(((bf16[384,1024]{0,1:T(8,128)(2,1)}), bf16[3072,1024]{0,1:T(8,128)(2,1)}) %all-gather.4.cloned.1.call-update) | async-done | bytes 6291472 | tf_op jit(solution)/shard_map/all_gather | solution.py:67
  138.4 8.6 %copy.39 = bf16[3072,1024]{1,0:T(8,128)(2,1)} copy(bf16[3072,1024]{0,1:T(8,128)(2,1)} %all-gather.4.cloned.1.call-done) | data formatting | bytes 12582912 | tf_op jit(solution)/shard_map/all_gather | solution.py:67
  147.1 8.6 %gather_fusion.1 = bf16[1024,1024]{1,0:T(8,128)(2,1)S(1)} fusion(bf16[3072,1024]{1,0:T(8,128)(2,1)} %copy.39, s32[1024]{0:T(1024)S(1)} %broadcast_clamp_fusion), kind=kCustom, calls=%fused_computation.1 | custom fusion | bytes 4198400 | tf_op jit(solution)/shard_map/jit(_take)/gather | solution.py:31
  155.6 2.6 copy.40
  158.2 2.2 select_convert_fusion
  161.5 3.5 collective-permute-start
  165.1 1.3 copy.41
  167.6 20.9 %collective-permute-done = bf16[512,1024]{0,1:T(8,128)(2,1)} collective-permute-done((bf16[512,1024]{0,1:T(8,128)(2,1)}, bf16[512,1024]{0,1:T(8,128)(2,1)}, u32[]{:S(2)}, u32[]{:S(2)}) %collective-permute-start) | collective-permute-done | bytes 1048608 | tf_op jit(solution)/shard_map/ppermute | solution.py:12
  188.4 1.7 convert_add_fusion
  190.1 1.3 copy-done.2
  191.7 3.6 collective-permute-start.1
  195.3 11.0 %collective-permute-done.1 = bf16[512,512]{0,1:T(8,128)(2,1)S(1)} collective-permute-done((bf16[512,512]{0,1:T(8,128)(2,1)S(1)}, bf16[512,512]{0,1:T(8,128)(2,1)S(1)}, u32[]{:S(2)}, u32[]{:S(2)}) %collective-permute-start.1) | collective-permute-done | bytes 524320 | tf_op jit(solution)/shard_map/ppermute | solution.py:12
  207.8 1.2 convert_select_fusion
  209.1 83.1 %all-reduce.6.cloned.1.call-done = bf16[512,512]{0,1:T(8,128)(2,1)} async-done(((bf16[512,512]{0,1:T(8,128)(2,1)}), bf16[512,512]{0,1:T(8,128)(2,1)}) %all-reduce.6.cloned.1.call-update) | async-done | bytes 524304 | tf_op jit(solution)/shard_map/psum | solution.py:17
  292.2 2.2 convert_select_fusion.2
  294.4 1.6 copy.42
  295.9 1.3 fusion.16
  298.3 11.7 %cholesky.103 = f32[128,128]{1,0:T(8,128)S(1)} custom-call(f32[128,128]{1,0:T(8,128)S(1)} %cholesky.263), custom_call_target="Cholesky" | custom-call | tf_op jit(solution)/shard_map/jit(cholesky)/cholesky | solution.py:39
  310.0 9.8 %custom-call.30 = f32[1,128,128]{1,2,0:T(8,128)S(1)} custom-call(f32[1,128,128]{2,1,0:T(8,128)S(1)} %get-tuple-element.59), custom_call_target="InvertDiagBlocksLowerTriangular" | custom-call | tf_op jit(solution)/shard_map/jit(cholesky)/cholesky | solution.py:39
  319.8 1.2 fusion.40
  321.1 1.3 convolution_subtract_fusion
  322.4 11.7 %cholesky.215 = f32[128,128]{1,0:T(8,128)S(1)} custom-call(f32[128,128]{1,0:T(8,128)S(1)} %cholesky.267), custom_call_target="Cholesky" | custom-call | tf_op jit(solution)/shard_map/jit(cholesky)/cholesky | solution.py:39
  335.7 10.6 %custom-call.31 = f32[1,128,128]{1,2,0:T(8,128)} custom-call(f32[1,128,128]{2,1,0:T(8,128)S(1)} %get-tuple-element.57), custom_call_target="InvertDiagBlocksLowerTriangular" | custom-call | tf_op jit(solution)/shard_map/jit(cholesky)/cholesky | solution.py:39
  349.3 1.5 convolution_subtract_fusion.1
  350.8 11.7 %cholesky.236 = f32[128,128]{1,0:T(8,128)S(1)} custom-call(f32[128,128]{1,0:T(8,128)S(1)} %cholesky.272), custom_call_target="Cholesky" | custom-call | tf_op jit(solution)/shard_map/jit(cholesky)/cholesky | solution.py:39
  362.6 9.8 %custom-call.32 = f32[1,128,128]{1,2,0:T(8,128)S(1)} custom-call(f32[1,128,128]{2,1,0:T(8,128)S(1)} %get-tuple-element.55), custom_call_target="InvertDiagBlocksLowerTriangular" | custom-call | tf_op jit(solution)/shard_map/jit(cholesky)/cholesky | solution.py:39
  372.7 1.3 convolution_subtract_fusion.2
  374.1 11.9 %cholesky.253 = f32[128,128]{1,0:T(8,128)S(1)} custom-call(f32[128,128]{1,0:T(8,128)S(1)} %convolution_subtract_fusion.2), custom_call_target="Cholesky" | custom-call | tf_op jit(solution)/shard_map/jit(cholesky)/cholesky | solution.py:39
  392.3 14.3 %while.1 = (s32[]{:T(128)}, f32[512,512]{0,1:T(8,128)}, s32[4,2]{0,1:T(2,128)S(1)}, f32[4,128,128]{2,1,0:T(8,128)}, s32[]{:T(128)}) while((s32[]{:T(128)}, f32[512,512]{0,1:T(8,128)}, s32[4,2]{0,1:T(2,128)S(1)}, f32[4,128,128]{2,1,0:T(8,128)}, s32[]{:T(128)}) %tuple.40), condition=%wide.while_cond, body=%wide.while_body.sunk | while | flops 2 | bytes 393829 | solution.py:40
  392.9 2.3 dynamic-slice.7
  396.5 2.3 dynamic-slice.7
  400.1 2.3 dynamic-slice.7
  403.7 2.2 dynamic-slice.7
  406.6 40.1 %custom-call.33 = f32[4,128,128]{1,2,0:T(8,128)S(1)} custom-call(f32[4,128,128]{2,1,0:T(8,128)} %get-tuple-element.9), custom_call_target="InvertDiagBlocksLowerTriangular" | custom-call | tf_op jit(solution)/shard_map/triangular_solve | solution.py:40
  447.4 1.5 fusion.47
  449.5 1.7 fusion.9
  451.8 2.1 fusion
  454.5 1.6 maximum_select_fusion
  456.2 88.2 %all-reduce.8.cloned.1.call-done = f32[1024,512]{0,1:T(8,128)} async-done(((f32[1024,512]{0,1:T(8,128)}), f32[1024,512]{0,1:T(8,128)}) %all-reduce.8.cloned.1.call-update) | async-done | bytes 2097168 | tf_op jit(solution)/shard_map/psum | solution.py:17
  544.4 1.7 convert_element_type.58
  549.7 2.7 copy.55
  552.3 84.4 %all-reduce.10.cloned.1.call-done = (bf16[512,512]{0,1:T(8,128)(2,1)}, bf16[512,512]{0,1:T(8,128)(2,1)}) async-done(((bf16[512,512]{0,1:T(8,128)(2,1)}, bf16[512,512]{0,1:T(8,128)(2,1)}), (bf16[512,512]{0,1:T(8,128)(2,1)}, bf16[512,512]{0,1:T(8,128)(2,1)})) %all-reduce.10.cloned.1.call-update) | async-done | bytes 1048592 | tf_op jit(solution)/shard_map/psum | solution.py:17
  636.7 3.0 fusion.6
  639.7 2.3 copy.56
  (99 shorter events, 25.7 us)
Async XLA Ops:
  7.2 2.0 copy-start
  7.2 48.3 %all-gather.6.cloned.1.call-start = ((), (), s32[]{:S(2)}) async-start(), calls=%async_computation.3 | async-start | bytes 2654208 | tf_op jit(solution)/shard_map/all_gather | solution.py:65
  9.1 129.3 %all-gather.4.cloned.1.call-start = ((), (), s32[]{:S(2)}) async-start(), calls=%async_computation | async-start | bytes 7077888 | tf_op jit(solution)/shard_map/all_gather | solution.py:67
  62.4 229.7 %all-reduce.6.cloned.1.call-start = ((), (), s32[]{:S(2)}) async-start(), calls=%async_computation.1 | async-start | bytes 1048576 | tf_op jit(solution)/shard_map/psum | solution.py:17
  160.4 4.7 copy-start.7
  160.4 6.0 copy-start.8
  161.5 26.9 %collective-permute-start = (bf16[512,1024]{0,1:T(8,128)(2,1)}, bf16[512,1024]{0,1:T(8,128)(2,1)}, u32[]{:S(2)}, u32[]{:S(2)}) collective-permute-start(bf16[512,1024]{0,1:T(8,128)(2,1)} %broadcast_select_fusion), channel_id=1, source_target_pairs={{0,64},{64,0},{128,192},{192,128},{256,320},{320,256},{384,448},{4... | collective-permute-start | bytes 3145736 | tf_op jit(solution)/shard_map/ppermute | solution.py:12
  167.6 23.9 %copy-start.4 = (f32[1,512,512]{1,2,0:T(8,128)S(1)}, f32[1,512,512]{1,2,0:T(8,128)}, u32[]{:S(2)}) copy-start(f32[1,512,512]{1,2,0:T(8,128)} %copy.41) | copy-start | bytes 3145732
  190.1 1.4 copy-start.2
  191.7 14.5 %collective-permute-start.1 = (bf16[512,512]{0,1:T(8,128)(2,1)S(1)}, bf16[512,512]{0,1:T(8,128)(2,1)S(1)}, u32[]{:S(2)}, u32[]{:S(2)}) collective-permute-start(bf16[512,512]{0,1:T(8,128)(2,1)S(1)} %get-tuple-element.44), channel_id=1, source_target_pairs={{0,64},{64,0},{128,192},{192,128},{256,320},{320,256},{384,448},{4... | collective-permute-start | bytes 1572872 | tf_op jit(solution)/shard_map/ppermute | solution.py:12
  206.3 1.6 copy-start.6
  207.3 337.1 %all-reduce.8.cloned.1.call-start = ((), (), s32[]{:S(2)}) async-start(), calls=%async_computation.2 | async-start | bytes 4194304 | tf_op jit(solution)/shard_map/psum | solution.py:17
  297.3 1.0 copy-start.5
  456.1 180.6 %all-reduce.10.cloned.1.call-start = ((), (), s32[]{:S(2)}) async-start(), calls=%async_computation.4 | async-start | bytes 2097152 | tf_op jit(solution)/shard_map/psum | solution.py:17
  546.2 2.3 copy-start.1
  549.6 87.1 %copy-start.3 = (f32[512,1024]{0,1:T(8,128)S(1)}, f32[512,1024]{0,1:T(8,128)}, u32[]{:S(2)}) copy-start(f32[512,1024]{0,1:T(8,128)} %copy-done.2) | copy-start | bytes 6291460
Sparse Core Ops, SparseCore 0:
  10.7 44.7 all-gather.5
  62.6 75.8 all-gather.3
  207.4 84.7 all-reduce.5
  456.2 88.1 all-reduce.7
  547.4 89.2 all-reduce.9
where the time goes:
time: 655 us; the launch traced here: 649 us
  waiting for transfers between devices  409 us (62%)
  other arithmetic  141 us (22%)
  local copies, waits for them, and re-layouts  56 us (9%)
  matrix products  17.5 us (3%)
  between operations  17.1 us (3%)
  starting transfers between devices  7.77 us (1%)
    psum x3, waiting for transfers between devices, spread(): return lax.psum(kept, axis)  256 us
    another operation x15, other arithmetic, solve_rows(): chol_lower = jnp.linalg.cholesky(square)  79.9 us
    all_gather x1, waiting for transfers between devices, on_device(): lax.all_gather(strip.astype(jnp.bfloat16), 'row', axis=0, tiled=True)  75.8 us
    all_gather x1, waiting for transfers between devices, on_device(): lax.all_gather(child_block, 'col', axis=1, tiled=True)  45.9 us
    another operation x3, other arithmetic, solve_rows(): lax.linalg.triangular_solve(chol_lower, columns, left_side=False, lower=T...  41.2 us
    ppermute x2, waiting for transfers between devices, from_partner(): lax.ppermute(shard, axis, [(i, i ^ 1 << apart) for i in range(lax.axis_si...  31.8 us
    gather x3, local copies, waits for them, and re-layouts, pick_entries(): jnp.take(shard_piece, jnp.clip(sources, 0, extent - 1), axis=along)  16.9 us
    another operation x20, local copies, waits for them, and re-layouts  14.2 us
  transfers between devices with their start and end apart: 7, of which 7 were waited for; matrix products, arithmetic and copies ran while one was open for 1% of the time, Pallas kernels for 0%

commit v1 on v0

--- a/solution.py
+++ b/solution.py
@@ -14,7 +14,8 @@
 
 def spread(value, axis, source):
     kept = jnp.where(lax.axis_index(axis) == source, value, 0).astype(value.dtype)
-    return lax.psum(kept, axis)
+    answer_boxes = lambda in_array, axis_key: jax.lax.all_gather(in_array, axis_key).sum(axis=0)
+    return answer_boxes(kept, axis)
 
 
 def source_index(block_list, targets):

time: 655 us -> 749 us (1.14)
  the two profiles are of different devices: /device:TPU:16 before, /device:TPU:1 now
where the time goes in v1:
time: 749 us; the launch traced here: 741 us
  waiting for transfers between devices  472 us (63%)
  other arithmetic  156 us (21%)
  local copies, waits for them, and re-layouts  73.3 us (10%)
  between operations  17.6 us (2%)
  matrix products  15.3 us (2%)
    all_gather x4, waiting for transfers between devices, spread(): jax.lax.all_gather(in_array, axis_key).sum(axis=0)  318 us
    another operation x15, other arithmetic, solve_rows(): chol_lower = jnp.linalg.cholesky(square)  80.1 us
    all_gather x1, waiting for transfers between devices, on_device(): lax.all_gather(strip.astype(jnp.bfloat16), 'row', axis=0, tiled=True)  75 us
    all_gather x1, waiting for transfers between devices, on_device(): lax.all_gather(child_block, 'col', axis=1, tiled=True)  47.6 us
    another operation x3, other arithmetic, solve_rows(): lax.linalg.triangular_solve(chol_lower, columns, left_side=False, lower=T...  41.2 us
    ppermute x2, waiting for transfers between devices, from_partner(): lax.ppermute(shard, axis, [(i, i ^ 1 << apart) for i in range(lax.axis_si...  30.6 us
    unnamed x25, local copies, waits for them, and re-layouts  22.6 us
    reduce_sum x4, other arithmetic, spread(): jax.lax.all_gather(in_array, axis_key).sum(axis=0)  18.9 us
  transfers between devices with their start and end apart: 8, of which 8 were waited for; matrix products, arithmetic and copies ran while one was open for 2% of the time, Pallas kernels for 0%

profile of v1, /device:TPU:1, one launch (start us, length us, event | category | flops | bytes accessed | tf_op | source)
XLA Modules:
  0.0 741.0 jit_solution(13909162795094355962)
XLA Ops:
  7.2 1.8 copy.85
  9.6 47.6 %all-gather.15.cloned.1.call-done = bf16[1,384,3072]{1,2,0:T(8,128)(2,1)} async-done(((bf16[1,384,384]{1,2,0:T(8,128)(2,1)}), bf16[1,384,3072]{1,2,0:T(8,128)(2,1)}) %all-gather.15.cloned.1.call-update) | async-done | bytes 2359312 | tf_op jit(solution)/shard_map/all_gather | solution.py:66
  57.1 5.7 gather_fusion
  64.3 75.0 %all-gather.11.cloned.1.call-done = bf16[3072,1024]{0,1:T(8,128)(2,1)} async-done(((bf16[384,1024]{0,1:T(8,128)(2,1)}), bf16[3072,1024]{0,1:T(8,128)(2,1)}) %all-gather.11.cloned.1.call-update) | async-done | bytes 6291472 | tf_op jit(solution)/shard_map/all_gather | solution.py:68
  139.3 8.6 %copy.86 = bf16[3072,1024]{1,0:T(8,128)(2,1)} copy(bf16[3072,1024]{0,1:T(8,128)(2,1)} %all-gather.11.cloned.1.call-done) | data formatting | bytes 12582912 | tf_op jit(solution)/shard_map/all_gather | solution.py:68
  147.9 8.6 %gather_fusion.1 = bf16[1024,1024]{1,0:T(8,128)(2,1)S(1)} fusion(bf16[3072,1024]{1,0:T(8,128)(2,1)} %copy.86, s32[1024]{0:T(1024)S(1)} %broadcast_clamp_fusion), kind=kCustom, calls=%fused_computation.1 | custom fusion | bytes 4198400 | tf_op jit(solution)/shard_map/jit(_take)/gather | solution.py:32
  156.5 2.6 copy.87
  159.0 2.2 select_convert_fusion
  162.3 3.3 collective-permute-start
  168.2 20.2 %collective-permute-done = bf16[512,1024]{0,1:T(8,128)(2,1)} collective-permute-done((bf16[512,1024]{0,1:T(8,128)(2,1)}, bf16[512,1024]{0,1:T(8,128)(2,1)}, u32[]{:S(2)}, u32[]{:S(2)}) %collective-permute-start) | collective-permute-done | bytes 1048608 | tf_op jit(solution)/shard_map/ppermute | solution.py:12
  188.4 1.7 convert_add_fusion
  190.1 1.3 copy-done.2
  191.7 3.3 collective-permute-start.1
  195.0 10.4 %collective-permute-done.1 = bf16[512,512]{0,1:T(8,128)(2,1)S(1)} collective-permute-done((bf16[512,512]{0,1:T(8,128)(2,1)S(1)}, bf16[512,512]{0,1:T(8,128)(2,1)S(1)}, u32[]{:S(2)}, u32[]{:S(2)}) %collective-permute-start.1) | collective-permute-done | bytes 524320 | tf_op jit(solution)/shard_map/ppermute | solution.py:12
  208.3 56.6 %all-gather.17.cloned.1.call-done = bf16[4096,512]{0,1:T(8,128)(2,1)} async-done(((bf16[512,512]{0,1:T(8,128)(2,1)}), bf16[4096,512]{0,1:T(8,128)(2,1)}) %all-gather.17.cloned.1.call-update) | async-done | bytes 4194320 | tf_op jit(solution)/shard_map/all_gather | solution.py:17
  265.0 4.4 copy.116
  269.4 3.3 bitcast_reduce_fusion.2
  273.9 2.5 copy.90
  276.4 1.5 fusion.9
  278.9 11.7 %cholesky.103 = f32[128,128]{1,0:T(8,128)S(1)} custom-call(f32[128,128]{1,0:T(8,128)S(1)} %cholesky.263), custom_call_target="Cholesky" | custom-call | tf_op jit(solution)/shard_map/jit(cholesky)/cholesky | solution.py:40
  290.6 9.8 %custom-call.30 = f32[1,128,128]{1,2,0:T(8,128)S(1)} custom-call(f32[1,128,128]{2,1,0:T(8,128)S(1)} %get-tuple-element.69), custom_call_target="InvertDiagBlocksLowerTriangular" | custom-call | tf_op jit(solution)/shard_map/jit(cholesky)/cholesky | solution.py:40
  303.0 12.1 %cholesky.215 = f32[128,128]{1,0:T(8,128)S(1)} custom-call(f32[128,128]{1,0:T(8,128)S(1)} %cholesky.267), custom_call_target="Cholesky" | custom-call | tf_op jit(solution)/shard_map/jit(cholesky)/cholesky | solution.py:40
  316.7 10.4 %custom-call.31 = f32[1,128,128]{1,2,0:T(8,128)} custom-call(f32[1,128,128]{2,1,0:T(8,128)S(1)} %get-tuple-element.67), custom_call_target="InvertDiagBlocksLowerTriangular" | custom-call | tf_op jit(solution)/shard_map/jit(cholesky)/cholesky | solution.py:40
  330.1 1.5 convolution_subtract_fusion.1
  331.6 11.7 %cholesky.236 = f32[128,128]{1,0:T(8,128)S(1)} custom-call(f32[128,128]{1,0:T(8,128)S(1)} %cholesky.272), custom_call_target="Cholesky" | custom-call | tf_op jit(solution)/shard_map/jit(cholesky)/cholesky | solution.py:40
  343.5 9.8 %custom-call.32 = f32[1,128,128]{1,2,0:T(8,128)S(1)} custom-call(f32[1,128,128]{2,1,0:T(8,128)S(1)} %get-tuple-element.65), custom_call_target="InvertDiagBlocksLowerTriangular" | custom-call | tf_op jit(solution)/shard_map/jit(cholesky)/cholesky | solution.py:40
  353.6 1.3 convolution_subtract_fusion.2
  355.0 11.8 %cholesky.253 = f32[128,128]{1,0:T(8,128)S(1)} custom-call(f32[128,128]{1,0:T(8,128)S(1)} %convolution_subtract_fusion.2), custom_call_target="Cholesky" | custom-call | tf_op jit(solution)/shard_map/jit(cholesky)/cholesky | solution.py:40
  373.0 14.3 %while.1 = (s32[]{:T(128)}, f32[512,512]{0,1:T(8,128)}, s32[4,2]{0,1:T(2,128)S(1)}, f32[4,128,128]{2,1,0:T(8,128)}, s32[]{:T(128)}) while((s32[]{:T(128)}, f32[512,512]{0,1:T(8,128)}, s32[4,2]{0,1:T(2,128)S(1)}, f32[4,128,128]{2,1,0:T(8,128)}, s32[]{:T(128)}) %tuple.45), condition=%wide.while_cond, body=%wide.while_body.sunk | while | flops 2 | bytes 393829 | solution.py:41
  373.6 2.3 dynamic-slice.7
  377.2 2.3 dynamic-slice.7
  380.8 2.3 dynamic-slice.7
  384.4 2.2 dynamic-slice.7
  387.3 40.1 %custom-call.33 = f32[4,128,128]{1,2,0:T(8,128)S(1)} custom-call(f32[4,128,128]{2,1,0:T(8,128)} %get-tuple-element.9), custom_call_target="InvertDiagBlocksLowerTriangular" | custom-call | tf_op jit(solution)/shard_map/triangular_solve | solution.py:41
  428.1 1.5 fusion.48
  430.2 1.7 fusion.12
  432.5 2.1 fusion
  435.4 1.8 copy.102
  437.5 159.2 %all-gather.13.cloned.1.call-done = f32[8,1024,512]{2,1,0:T(8,128)} async-done(((f32[1,1024,512]{2,1,0:T(8,128)}), f32[8,1024,512]{2,1,0:T(8,128)}) %all-gather.13.cloned.1.call-update) | async-done | bytes 16777232 | tf_op jit(solution)/shard_map/all_gather | solution.py:17
  596.8 9.4 %reduce_sum.66 = f32[1024,512]{1,0:T(8,128)} reduce(f32[8,1024,512]{2,1,0:T(8,128)} %all-gather.13.cloned.1.call-done, f32[]{:T(128)} %constant.284.clone.1), dimensions={0}, to_apply=%region_13.14 | reduce | flops 3670016 | bytes 18874372 | tf_op jit(solution)/shard_map/reduce_sum | solution.py:17
  606.1 1.9 copy.103
  611.8 2.5 copy.107
  614.3 51.1 %all-gather.21.cloned.1.call-done = bf16[4096,512]{0,1:T(8,128)(2,1)} async-done(((bf16[512,512]{0,1:T(8,128)(2,1)}), bf16[4096,512]{0,1:T(8,128)(2,1)}) %all-gather.21.cloned.1.call-update) | async-done | bytes 4194320 | tf_op jit(solution)/shard_map/all_gather | solution.py:17
  665.4 4.4 copy.118
  669.8 3.1 bitcast_reduce_fusion
  672.9 51.1 %all-gather.19.cloned.1.call-done = bf16[4096,512]{0,1:T(8,128)(2,1)} async-done(((bf16[512,512]{0,1:T(8,128)(2,1)}), bf16[4096,512]{0,1:T(8,128)(2,1)}) %all-gather.19.cloned.1.call-update) | async-done | bytes 4194320 | tf_op jit(solution)/shard_map/all_gather | solution.py:17
  724.1 4.4 copy.117
  728.5 3.1 bitcast_reduce_fusion.1
  (112 shorter events, 36.0 us)
Async XLA Ops:
  7.2 2.0 copy-start
  7.2 50.0 %all-gather.15.cloned.1.call-start = ((), (), s32[]{:S(2)}) async-start(), calls=%async_computation.2 | async-start | bytes 2654208 | tf_op jit(solution)/shard_map/all_gather | solution.py:66
  9.1 130.2 %all-gather.11.cloned.1.call-start = ((), (), s32[]{:S(2)}) async-start(), calls=%async_computation | async-start | bytes 7077888 | tf_op jit(solution)/shard_map/all_gather | solution.py:68
  64.1 200.8 %all-gather.17.cloned.1.call-start = ((), (), s32[]{:S(2)}) async-start(), calls=%async_computation.3 | async-start | bytes 4718592 | tf_op jit(solution)/shard_map/all_gather | solution.py:17
  161.2 4.4 copy-start.7
  161.2 5.7 copy-start.8
  162.3 26.1 %collective-permute-start = (bf16[512,1024]{0,1:T(8,128)(2,1)}, bf16[512,1024]{0,1:T(8,128)(2,1)}, u32[]{:S(2)}, u32[]{:S(2)}) collective-permute-start(bf16[512,1024]{0,1:T(8,128)(2,1)} %broadcast_select_fusion), channel_id=1, source_target_pairs={{0,64},{64,0},{128,192},{192,128},{256,320},{320,256},{384,448},{4... | collective-permute-start | bytes 3145736 | tf_op jit(solution)/shard_map/ppermute | solution.py:12
  168.2 23.3 %copy-start.4 = (f32[1,512,512]{1,2,0:T(8,128)S(1)}, f32[1,512,512]{1,2,0:T(8,128)}, u32[]{:S(2)}) copy-start(f32[1,512,512]{1,2,0:T(8,128)} %copy.88) | copy-start | bytes 3145732
  190.1 1.4 copy-start.2
  191.7 13.7 %collective-permute-start.1 = (bf16[512,512]{0,1:T(8,128)(2,1)S(1)}, bf16[512,512]{0,1:T(8,128)(2,1)S(1)}, u32[]{:S(2)}, u32[]{:S(2)}) collective-permute-start(bf16[512,512]{0,1:T(8,128)(2,1)S(1)} %get-tuple-element.54), channel_id=1, source_target_pairs={{0,64},{64,0},{128,192},{192,128},{256,320},{320,256},{384,448},{4... | collective-permute-start | bytes 1572872 | tf_op jit(solution)/shard_map/ppermute | solution.py:12
  205.4 1.7 copy-start.6
  206.4 390.4 %all-gather.13.cloned.1.call-start = ((), (), s32[]{:S(2)}) async-start(), calls=%async_computation.1 | async-start | bytes 18874368 | tf_op jit(solution)/shard_map/all_gather | solution.py:17
  277.9 1.0 copy-start.5
  437.2 228.2 %all-gather.21.cloned.1.call-start = ((), (), s32[]{:S(2)}) async-start(), calls=%async_computation.5 | async-start | bytes 4718592 | tf_op jit(solution)/shard_map/all_gather | solution.py:17
  609.4 114.7 %all-gather.19.cloned.1.call-start = ((), (), s32[]{:S(2)}) async-start(), calls=%async_computation.4 | async-start | bytes 4718592 | tf_op jit(solution)/shard_map/all_gather | solution.py:17
  728.5 3.1 copy-start.3
  731.6 2.2 copy-start.1
Sparse Core Ops, SparseCore 0:
  10.7 46.4 all-gather.14
  64.3 74.9 all-gather.10
  206.5 58.3 all-gather.16
  437.4 159.3 all-gather.12
  609.5 55.8 all-gather.20
  667.4 56.6 all-gather.18
